TPU v7x, 32 devices: a whole 2x2x4 slice. The times are simulated.
32 devices in a mesh: dp: 16 (over z, x, core), tensor: 2 (over y).
Axes of the slice: x: 2, y: 2, z: 4, core: 2. Of those that a mesh axis runs over, the one named last changes fastest.
Arguments:
- hidden_in: bfloat16 [16384, 1024], P(('dp', 'tensor')), may hold values from -6 to 6
- positions: int32 [16384], P('dp'), may hold values from 0 to 1023, as said below
- gain_attention: float32 [1024], replicated, may hold values from 0.1 to 1.9
- gain_feedforward: float32 [1024], replicated, may hold values from 0.1 to 1.9
- gain_query: float32 [128], replicated, may hold values from 0.7 to 5
- gain_key: float32 [128], replicated, may hold values from 0.7 to 5
- query_proj: bfloat16 [1024, 2048], P('dp', 'tensor'), may hold values from -0.1875 to 0.1875
- key_proj: bfloat16 [1024, 1024], P('dp', 'tensor'), may hold values from -0.1875 to 0.1875
- value_proj: bfloat16 [1024, 1024], P('dp', 'tensor'), may hold values from -0.1875 to 0.1875
- out_proj: bfloat16 [2048, 1024], P(('tensor', 'dp')), may hold values from -3 to 3
- gate_proj: bfloat16 [1024, 3072], P('dp', 'tensor'), may hold values from -0.1875 to 0.1875
- up_proj: bfloat16 [1024, 3072], P('dp', 'tensor'), may hold values from -0.1875 to 0.1875
- down_proj: bfloat16 [3072, 1024], P(('tensor', 'dp')), may hold values from -0.21875 to 0.21875
- cotangent: bfloat16 [16384, 1024], P(('dp', 'tensor')), may hold values from -6 to 6
Outputs:
- hidden_out: bfloat16 [16384, 1024], P(('dp', 'tensor'))
- grad_hidden: float32 [16384, 1024], P(('dp', 'tensor'))
- attention_gain_grad: float32 [1024], replicated
- feedforward_gain_grad: float32 [1024], replicated
- query_gain_grad: float32 [128], replicated
- key_gain_grad: float32 [128], replicated
- query_grads: float32 [1024, 2048], P('dp', 'tensor')
- key_grads: float32 [1024, 1024], P('dp', 'tensor')
- value_grads: float32 [1024, 1024], P('dp', 'tensor')
- out_grads: float32 [2048, 1024], P(('tensor', 'dp'))
- gate_grads: float32 [1024, 3072], P('dp', 'tensor')
- up_grads: float32 [1024, 3072], P('dp', 'tensor')
- down_grads: float32 [3072, 1024], P(('tensor', 'dp'))
Inputs may be any that keep to these rules, and one draw needn't show every extreme that they name: Within each sequence of 1024 tokens the positions start at 0 and rise by one from token to token, except that they restart at 0 where a document begins; some sequence holds one document.
All inputs are finite; a program needn't handle non-finite values.
Results may differ from a plain program's by a relative error of at most 0.02.
The roundings to bfloat16 on the way count: a program that leaves them out, or rounds other values in their place, can miss the bound.
Values may be sent and summed in bfloat16 or wider, within the bound.
No kernel may reach another device: no remote copies, remote signals or barrier semaphores. Data moves between devices by JAX's collectives and lax.ppermute only.
A program may use at most 256 MiB of HBM per device.

v0:
```python
import math
import jax
import jax.numpy as jnp
from jax import lax
from jax.sharding import PartitionSpec as P

HD = 128
EPS = 1e-06
THETA = 1000000.0
BF = jnp.bfloat16
F32 = jnp.float32


def rotary_tables(positions, width):
    half_width = width // 2
    freq_index = jnp.arange(half_width).astype(F32)
    inverse_freq = jnp.exp(freq_index * (-2.0 * math.log(THETA) / width))
    angles = positions.astype(F32)[:, None] * inverse_freq[None, :]
    return (jnp.cos(angles)[:, None, :], jnp.sin(angles)[:, None, :])


def rotate(values, cosine_table, sine_table):
    half_width = values.shape[-1] // 2
    lower_half = values[..., :half_width]
    upper_half = values[..., half_width:]
    return jnp.concatenate(
        (
            lower_half * cosine_table - upper_half * sine_table,
            upper_half * cosine_table + lower_half * sine_table,
        ),
        -1,
    )


def rms_unit(values):
    inv_scale = lax.rsqrt(jnp.mean(values * values, -1, keepdims=True) + EPS)
    return (values * inv_scale, inv_scale)


def rms_back(grad_out, gain_vec, unit_vals, inv_scale):
    scaled_grad = grad_out * gain_vec
    return inv_scale * (
        scaled_grad - unit_vals * jnp.mean(scaled_grad * unit_vals, -1, keepdims=True)
    )


def matmul(left, right):
    return jnp.dot(left, right, preferred_element_type=F32)


def contract_rows(left, right):
    return lax.dot_general(left, right, (((0,), (0,)), ((), ())), preferred_element_type=F32)


def contract_cols(left, right):
    return lax.dot_general(left, right, (((1,), (1,)), ((), ())), preferred_element_type=F32)


def attend(query_b, key_b, value_b):
    length = query_b.shape[0]
    block_rows = min(length, 512)
    block_count = length // block_rows
    scale_qk = 1.0 / math.sqrt(query_b.shape[-1])
    outputs = []
    log_sums = []
    for block in range(block_count):
        row_start = block * block_rows
        key_end = row_start + block_rows
        query_block = query_b[row_start:key_end]
        scores = (
            jnp.einsum("qgrd,kgd->grqk", query_block, key_b[:key_end], preferred_element_type=F32)
            * scale_qk
        )
        causal = (row_start + jnp.arange(block_rows, dtype=jnp.int32))[:, None] >= jnp.arange(
            key_end, dtype=jnp.int32
        )[None, :]
        scores = jnp.where(causal, scores, -jnp.inf)
        top_score = jnp.max(scores, -1, keepdims=True)
        shifted = jnp.exp(scores - top_score)
        sum_exp = jnp.sum(shifted, -1, keepdims=True)
        probs_b = (shifted / sum_exp).astype(BF)
        outputs.append(
            jnp.einsum("grqk,kgd->qgrd", probs_b, value_b[:key_end], preferred_element_type=F32)
        )
        log_sums.append(top_score + jnp.log(sum_exp))
    return (jnp.concatenate(outputs, 0), log_sums)


def attend_back(query_b, key_b, value_b, grad_b, log_sums):
    length = query_b.shape[0]
    block_rows = min(length, 512)
    block_count = length // block_rows
    scale_qk = 1.0 / math.sqrt(query_b.shape[-1])
    key_acc = jnp.zeros(key_b.shape, F32)
    value_acc = jnp.zeros(key_b.shape, F32)
    grad_queries = []
    for block in range(block_count):
        row_start = block * block_rows
        key_end = row_start + block_rows
        query_block = query_b[row_start:key_end]
        grad_block = grad_b[row_start:key_end]
        keys_seen = key_b[:key_end]
        scores = (
            jnp.einsum("qgrd,kgd->grqk", query_block, keys_seen, preferred_element_type=F32)
            * scale_qk
        )
        causal = (row_start + jnp.arange(block_rows, dtype=jnp.int32))[:, None] >= jnp.arange(
            key_end, dtype=jnp.int32
        )[None, :]
        scores = jnp.where(causal, scores, -jnp.inf)
        probs = jnp.exp(scores - log_sums[block])
        probs_b = probs.astype(BF)
        grad_probs = jnp.einsum(
            "qgrd,kgd->grqk", grad_block, value_b[:key_end], preferred_element_type=F32
        )
        row_dot = jnp.sum(probs * grad_probs, -1, keepdims=True)
        grad_scores_b = (probs * (grad_probs - row_dot)).astype(BF)
        grad_queries.append(
            jnp.einsum("grqk,kgd->qgrd", grad_scores_b, keys_seen, preferred_element_type=F32)
            * scale_qk
        )
        key_acc = key_acc.at[:key_end].add(
            jnp.einsum("grqk,qgrd->kgd", grad_scores_b, query_block, preferred_element_type=F32)
            * scale_qk
        )
        value_acc = value_acc.at[:key_end].add(
            jnp.einsum("grqk,qgrd->kgd", probs_b, grad_block, preferred_element_type=F32)
        )
    return (jnp.concatenate(grad_queries, 0), key_acc, value_acc)


def all_sum(value, sizes):
    for axis, size in sizes:
        if size & size - 1:
            value = lax.psum(value, axis)
            continue
        step = 1
        while step < size:
            value = value + lax.ppermute(value, axis, [(i, i ^ step) for i in range(size)])
            step *= 2
    return value


def make_local(n_dp, n_tensor):
    paired = n_tensor == 2
    swap = [(0, 1), (1, 0)]

    def gather_rows(own):
        if paired:
            return jnp.concatenate((own, lax.ppermute(own, "tensor", swap)), 0)
        return lax.all_gather(own, "tensor", axis=0, tiled=True)

    def to_sequence(rows):
        if not paired:
            return rows
        half = rows.shape[0] // 2
        first = lax.axis_index("tensor") == 0
        return jnp.concatenate(
            (
                jnp.where(first, rows[:half], rows[half:]),
                jnp.where(first, rows[half:], rows[:half]),
            ),
            0,
        )

    def scatter_rows(part, operand):
        if paired:
            half = operand[0].shape[0] // 2
            sent = part(*(o[half:] for o in operand)).astype(BF)
            got = lax.ppermute(sent, "tensor", swap)
            return part(*(o[:half] for o in operand)) + got.astype(F32)
        return lax.psum_scatter(
            part(*operand).astype(BF), "tensor", scatter_dimension=0, tiled=True
        ).astype(F32)

    def local(
        hidden_in,
        positions,
        gain_attention,
        gain_feedforward,
        gain_query,
        gain_key,
        query_proj,
        key_proj,
        value_proj,
        out_proj,
        gate_proj,
        up_proj,
        down_proj,
        cotangent,
    ):
        length = positions.shape[0]
        own = hidden_in.shape[0]
        width = hidden_in.shape[1]
        heads_here = query_proj.shape[1] // HD
        groups_here = key_proj.shape[1] // HD
        width_query = heads_here * HD
        width_key = groups_here * HD
        width_qkv = width_query + 2 * width_key
        units = gate_proj.shape[1]
        shard_rows = query_proj.shape[0]
        shard_attn = jnp.concatenate(
            (query_proj, key_proj, value_proj, out_proj.reshape(shard_rows, -1)), 1
        )
        shard_mlp = jnp.concatenate((gate_proj, up_proj, down_proj.reshape(shard_rows, -1)), 1)
        full_attn = lax.all_gather(shard_attn, "dp", axis=0, tiled=True)
        full_mlp = lax.all_gather(shard_mlp, "dp", axis=0, tiled=True)
        proj_qkv = full_attn[:, :width_qkv]
        full_out = full_attn[:, width_qkv:].reshape(-1, width)
        full_gateup = full_mlp[:, : 2 * units]
        full_down = full_mlp[:, 2 * units :].reshape(-1, width)
        rows_hidden = gather_rows(hidden_in)
        rows_cot = gather_rows(cotangent)
        cosine_table, sine_table = rotary_tables(positions, HD)
        unit_rows, scale_rows = rms_unit(rows_hidden.astype(F32))
        rows_attn = (unit_rows * gain_attention).astype(BF)
        if paired:
            hidden_f, unit_attn, scale_attn = (
                hidden_in.astype(F32),
                unit_rows[:own],
                scale_rows[:own],
            )
        else:
            hidden_f = hidden_in.astype(F32)
            unit_attn, scale_attn = rms_unit(hidden_f)
        projected = to_sequence(matmul(rows_attn, proj_qkv))
        query_raw = projected[:, :width_query].reshape(length, heads_here, HD)
        key_raw = projected[:, width_query : width_query + width_key].reshape(
            length, groups_here, HD
        )
        value_b = (
            projected[:, width_query + width_key :].astype(BF).reshape(length, groups_here, HD)
        )
        query_unit, query_scale = rms_unit(query_raw)
        key_unit, key_scale = rms_unit(key_raw)
        query_b = (
            rotate(query_unit * gain_query, cosine_table, sine_table)
            .astype(BF)
            .reshape(length, groups_here, heads_here // groups_here, HD)
        )
        key_b = rotate(key_unit * gain_key, cosine_table, sine_table).astype(BF)
        heads_out, log_sums = attend(query_b, key_b, value_b)
        heads_b = to_sequence(heads_out.reshape(length, width_query).astype(BF))
        resid = hidden_f + scatter_rows(lambda h: matmul(h, full_out), (heads_b,))
        unit_mlp, scale_mlp = rms_unit(resid)
        rows_mlp = gather_rows((unit_mlp * gain_feedforward).astype(BF))
        gate_val = matmul(rows_mlp, full_gateup[:, :units])
        up_val = matmul(rows_mlp, full_gateup[:, units:])
        sigmoid_gate = jax.nn.sigmoid(gate_val)
        active_b = (gate_val * sigmoid_gate * up_val).astype(BF)
        output_b = (resid + scatter_rows(lambda a: matmul(a, full_down), (active_b,))).astype(BF)
        grad_active = contract_cols(rows_cot, full_down)
        grad_gate_b = (
            grad_active * up_val * sigmoid_gate * (1.0 + gate_val * (1.0 - sigmoid_gate))
        ).astype(BF)
        grad_up_b = (grad_active * gate_val * sigmoid_gate).astype(BF)
        grad_normed_mlp = scatter_rows(
            lambda g, u: contract_cols(g, full_gateup[:, :units])
            + contract_cols(u, full_gateup[:, units:]),
            (grad_gate_b, grad_up_b),
        )
        grad_mlp_w = jnp.concatenate(
            (
                contract_rows(rows_mlp, grad_gate_b).astype(BF),
                contract_rows(rows_mlp, grad_up_b).astype(BF),
                contract_rows(active_b, rows_cot).astype(BF).reshape(width, -1),
            ),
            1,
        )
        sent_mlp = lax.psum_scatter(grad_mlp_w, "dp", scatter_dimension=0, tiled=True)
        term_feedforward = jnp.sum(grad_normed_mlp * unit_mlp, 0)
        grad_resid = cotangent.astype(F32) + rms_back(
            grad_normed_mlp, gain_feedforward, unit_mlp, scale_mlp
        )
        rows_resid = gather_rows(grad_resid.astype(BF))
        grad_heads_b = to_sequence(contract_cols(rows_resid, full_out).astype(BF)).reshape(
            length, groups_here, heads_here // groups_here, HD
        )
        grad_qrot, grad_krot, grad_value = attend_back(
            query_b, key_b, value_b, grad_heads_b, log_sums
        )
        grad_qnormed = rotate(grad_qrot.reshape(length, heads_here, HD), cosine_table, -sine_table)
        grad_knormed = rotate(grad_krot, cosine_table, -sine_table)
        term_query = jnp.sum(grad_qnormed * query_unit, (0, 1))
        term_key = jnp.sum(grad_knormed * key_unit, (0, 1))
        grad_qkv_b = to_sequence(
            jnp.concatenate(
                (
                    rms_back(grad_qnormed, gain_query, query_unit, query_scale).reshape(
                        length, width_query
                    ),
                    rms_back(grad_knormed, gain_key, key_unit, key_scale).reshape(
                        length, width_key
                    ),
                    grad_value.reshape(length, width_key),
                ),
                1,
            ).astype(BF)
        )
        grad_attn_w = jnp.concatenate(
            (
                contract_rows(rows_attn, grad_qkv_b).astype(BF),
                contract_rows(heads_b, rows_resid).astype(BF).reshape(width, -1),
            ),
            1,
        )
        sent_attn = lax.psum_scatter(grad_attn_w, "dp", scatter_dimension=0, tiled=True)
        grad_normed_attn = scatter_rows(lambda g: contract_cols(g, proj_qkv), (grad_qkv_b,))
        term_attention = jnp.sum(grad_normed_attn * unit_attn, 0)
        grad_hidden = grad_resid + rms_back(grad_normed_attn, gain_attention, unit_attn, scale_attn)
        terms = all_sum(
            jnp.concatenate((term_attention, term_feedforward, term_query, term_key)).reshape(
                -1, HD
            ),
            (("tensor", n_tensor), ("dp", n_dp)),
        ).reshape(-1)
        sent_attn = sent_attn.astype(F32)
        sent_mlp = sent_mlp.astype(F32)
        return (
            output_b,
            grad_hidden,
            terms[:width],
            terms[width : 2 * width],
            terms[2 * width : 2 * width + HD],
            terms[2 * width + HD :],
            sent_attn[:, :width_query],
            sent_attn[:, width_query : width_query + width_key],
            sent_attn[:, width_query + width_key : width_qkv],
            sent_attn[:, width_qkv:].reshape(out_proj.shape),
            sent_mlp[:, :units],
            sent_mlp[:, units : 2 * units],
            sent_mlp[:, 2 * units :].reshape(down_proj.shape),
        )

    return local


def solution(mesh):
    rows = P(("dp", "tensor"), None)
    cut = P("dp", "tensor")
    stacked = P(("tensor", "dp"), None)
    return jax.shard_map(
        make_local(mesh.shape["dp"], mesh.shape["tensor"]),
        mesh=mesh,
        in_specs=(
            rows,
            P("dp"),
            P(),
            P(),
            P(),
            P(),
            cut,
            cut,
            cut,
            stacked,
            cut,
            cut,
            stacked,
            rows,
        ),
        out_specs=(rows, rows, P(), P(), P(), P(), cut, cut, cut, stacked, cut, cut, stacked),
        check_vma=False,
    )
```

profile of v0, /device:TPU:0, one launch (start us, length us, event | category | flops | bytes accessed | tf_op | source)
XLA Modules:
  0.0 633.6 jit_solution(4155793221985874017)
XLA Ops:
  20.3 18.2 %collective-permute-done = bf16[512,1024]{1,0:T(8,128)(2,1)S(1)} collective-permute-done((bf16[512,1024]{1,0:T(8,128)(2,1)S(1)}, bf16[512,1024]{1,0:T(8,128)(2,1)S(1)}, u32[]{:S(2)}, u32[]{:S(2)}) %collective-permute-start) | collective-permute-done | bytes 1048608 | tf_op jit(solution)/shard_map/ppermute | solution.py:150
  39.0 36.1 %all-gather.3.cloned.1.call-done = bf16[1024,3072]{1,0:T(8,128)(2,1)} async-done(((bf16[64,3072]{1,0:T(8,128)(2,1)}), bf16[1024,3072]{1,0:T(8,128)(2,1)}) %all-gather.3.cloned.1.call-update) | async-done | bytes 6291472 | tf_op jit(solution)/shard_map/all_gather | solution.py:206
  75.0 10.0 %fusion.36 = f32[1024,2048]{1,0:T(8,128)} fusion(bf16[1024,3072]{1,0:T(8,128)(2,1)} %all-gather.3.cloned.1.call-done, f32[1024]{0:T(1024)S(1)} %copy-done.74, f32[1024]{0:T(1024)S(1)} %add_rsqrt_fusion.2, bf16[512,1024]{1,0:T(8,128)(2,1)S(1)} %collective-permute-done, bf16[512,1024]{1,0:T(8,128)(2,1)S(1)} %copy-done.40), kind=kOutput, calls=%fused_computation.77 | convolution fusion | flops 4302307328 | bytes 14688256 | tf_op jit(solution)/shard_map/dot_general | solution.py:48
  125.7 7.5 %fusion.135 = (f32[4,2,512]{2,1,0:T(2,128)S(1)}, f32[4,2,512,1024]{2,3,1,0:T(8,128)}) fusion(bf16[512,4,2,128]{3,0,2,1:T(8,128)(2,1)S(1)} %bitcast.234, bf16[1024,4,64]{2,0,1:T(8,128)(2,1)S(1)} %get-tuple-element.107, bf16[1024,4,64]{2,0,1:T(8,128)(2,1)S(1)} %get-tuple-element.106, pred[512,1024]{0,1:T(8,128)(4,1)S(1)} %copy-done.58), kind=kOutput, calls=%fused_computation.226 | convolution fusion | flops 1088417792 | bytes 19415040 | tf_op jit(solution)/shard_map/qgrd,kgd->grqk/dot_general | solution.py:71
  133.2 8.3 %fusion.3 = f32[4,2,512]{2,1,0:T(2,128)S(1)} fusion(f32[4,2,512,1024]{2,3,1,0:T(8,128)} %get-tuple-element.129, f32[4,2,512]{2,1,0:T(2,128)S(1)} %get-tuple-element.128), kind=kLoop, calls=%fused_computation.9 | loop fusion | flops 8384512 | bytes 16809984 | tf_op jit(solution)/shard_map/reduce_sum | solution.py:80
  141.6 7.8 %fusion.80 = bf16[4,128,2,512]{3,1,2,0:T(8,128)(2,1)S(1)} fusion(f32[4,2,512,1024]{2,3,1,0:T(8,128)} %get-tuple-element.129, f32[4,2,512]{2,1,0:T(2,128)S(1)} %fusion.3, f32[4,2,512]{2,1,0:T(2,128)S(1)} %get-tuple-element.128, bf16[1024,4,128,1]{2,1,0,3:T(4,128)(2,1)S(1)} %bitcast.237), kind=kOutput, calls=%fused_computation.156 | convolution fusion | flops 1086849024 | bytes 18907136 | tf_op jit(solution)/shard_map/grqk,kgd->qgrd/dot_general | solution.py:83
  157.6 24.0 %collective-permute-done.1 = bf16[512,1024]{1,0:T(8,128)(2,1)S(1)} collective-permute-done((bf16[512,1024]{1,0:T(8,128)(2,1)S(1)}, bf16[512,1024]{1,0:T(8,128)(2,1)S(1)}, u32[]{:S(2)}, u32[]{:S(2)}) %collective-permute-start.1) | collective-permute-done | bytes 1048608 | tf_op jit(solution)/shard_map/ppermute | solution.py:170
  188.9 15.2 %collective-permute-done.4 = bf16[512,1024]{1,0:T(8,128)(2,1)S(1)} collective-permute-done((bf16[512,1024]{1,0:T(8,128)(2,1)S(1)}, bf16[512,1024]{1,0:T(8,128)(2,1)S(1)}, u32[]{:S(2)}, u32[]{:S(2)}) %collective-permute-start.4) | collective-permute-done | bytes 1048608 | tf_op jit(solution)/shard_map/ppermute | solution.py:150
  208.8 5.9 reshape.389
  214.7 8.8 %fusion.136 = f32[1024,1536]{1,0:T(8,128)} fusion(bf16[1024,1024]{1,0:T(8,128)(2,1)} %constant_dynamic-update-slice_fusion, bf16[1536,1024]{1,0:T(8,128)(2,1)} %reshape.389), kind=kOutput, calls=%fused_computation.227 | convolution fusion | flops 3221225472 | bytes 11534336 | tf_op jit(solution)/shard_map/dot_general | solution.py:56
  225.9 8.6 %fusion.42 = f32[1024,1536]{1,0:T(8,128)} fusion(bf16[1024,4608]{1,0:T(8,128)(2,1)} %all-gather.5.cloned.1.call-done, bf16[512,1024]{1,0:T(8,128)(2,1)} %collective-permute-done.2, bf16[512,1024]{1,0:T(8,128)(2,1)} %multiply_convert_fusion.4), kind=kOutput, calls=%fused_computation.83 | convolution fusion | flops 3225419776 | bytes 11534336 | tf_op jit(solution)/shard_map/dot_general | solution.py:48
  234.5 10.6 %multiply_convert_fusion.1 = (bf16[1024,1536]{1,0:T(8,128)(2,1)S(1)}, bf16[1024,1536]{1,0:T(8,128)(2,1)}, bf16[1024,1536]{1,0:T(8,128)(2,1)S(1)}) fusion(f32[1024,1536]{1,0:T(8,128)} %fusion.136, f32[1024,1536]{1,0:T(8,128)} %fusion.42, bf16[1024,4608]{1,0:T(8,128)(2,1)S(1)} %bitcast.242, bf16[512,1024]{1,0:T(8,128)(2,1)} %collective-permute-done.2, ...), kind=kOutput, calls=%fused_computation.34 | convolution fusion | flops 3250585600 | bytes 27262976 | tf_op jit(solution)/shard_map/dot_general | solution.py:48
  252.2 21.1 %collective-permute-done.5 = bf16[512,1024]{1,0:T(8,128)(2,1)S(1)} collective-permute-done((bf16[512,1024]{1,0:T(8,128)(2,1)S(1)}, bf16[512,1024]{1,0:T(8,128)(2,1)S(1)}, u32[]{:S(2)}, u32[]{:S(2)}) %collective-permute-start.5) | collective-permute-done | bytes 1048608 | tf_op jit(solution)/shard_map/ppermute | solution.py:170
  281.0 20.6 %collective-permute-done.6 = bf16[512,1024]{1,0:T(8,128)(2,1)S(1)} collective-permute-done((bf16[512,1024]{1,0:T(8,128)(2,1)}, bf16[512,1024]{1,0:T(8,128)(2,1)S(1)}, u32[]{:S(2)}, u32[]{:S(2)}) %collective-permute-start.6) | collective-permute-done | bytes 1048608 | tf_op jit(solution)/shard_map/ppermute | solution.py:150
  319.2 11.2 %fusion = (f32[4,2,512]{2,1,0:T(2,128)}, f32[4,1024,512,2]{2,1,3,0:T(8,128)}) fusion(f32[4,2,512,1024]{2,3,1,0:T(8,128)S(1)} %bitcast.217, f32[4,2,512]{2,1,0:T(2,128)} %bitcast.246, bf16[512,4,2,128]{0,3,2,1:T(8,128)(2,1)} %bitcast.230, bf16[1024,4,128,1]{2,1,0,3:T(4,128)(2,1)} %bitcast.236), kind=kOutput, calls=%fused_computation.2 | convolution fusion | flops 1086320640 | bytes 35684352 | tf_op jit(solution)/shard_map/qgrd,kgd->grqk/dot_general | solution.py:113
  330.5 8.4 %fusion.2 = bf16[4,2,512,1024]{2,3,1,0:T(8,128)(2,1)S(1)} fusion(f32[4,1024,512,2]{2,1,3,0:T(8,128)} %get-tuple-element.136, f32[4,2,512,1024]{2,3,1,0:T(8,128)S(1)} %bitcast.217, f32[4,2,512]{2,1,0:T(2,128)} %get-tuple-element.135, f32[4,2,512]{2,1,0:T(2,128)} %bitcast.247), kind=kLoop, calls=%fused_computation.4 | loop fusion | flops 16777216 | bytes 41975808 | tf_op jit(solution)/shard_map/convert_element_type | solution.py:117
  356.0 17.1 %multiply_reduce_fusion = (f32[1024,8]{1,0:T(8,128)S(1)}, f32[1024,8,128]{2,1,0:T(8,128)}) fusion(f32[1024,8,128]{2,1,0:T(8,128)S(1)} %bitcast.221, f32[128]{0:T(128)S(1)} %copy-done.71, f32[1024,8]{1,0:T(8,128)S(1)} %copy-done.27, f32[1024,8,64]{2,1,0:T(8,128)S(1)} %get-tuple-element.89, f32[1024,8,64]{2,1,0:T(8,128)S(1)} %get-tuple-element.88), kind=kLoop, calls=%fused_computation.57 | loop fusion | flops 5234688 | bytes 12648960 | tf_op jit(solution)/shard_map/reduce_sum | solution.py:43
  381.7 9.9 %fusion.59 = bf16[1024,4,128]{0,2,1:T(8,128)(2,1)} fusion(f32[512,4,128]{0,2,1:T(8,128)} %fusion.100, bf16[512,4,2,128]{0,3,2,1:T(8,128)(2,1)S(1)} %bitcast.231, f32[4,2,512,1024]{2,3,1,0:T(8,128)} %get-tuple-element.129, f32[4,2,512]{2,1,0:T(2,128)S(1)} %bitcast.248), kind=kOutput, calls=%fused_computation.112 | convolution fusion | flops 1083179008 | bytes 19939328 | tf_op jit(solution)/shard_map/grqk,qgrd->kgd/dot_general | solution.py:127
  398.5 7.0 %fusion.22 = (f32[1024]{0:T(1024)S(1)}, bf16[1024,1024]{1,0:T(8,128)(2,1)S(1)}) fusion(f32[128,8,8,128]{3,2,1,0:T(8,128)} %bitcast.222, f32[128,8,8,128]{3,2,1,0:T(8,128)S(1)} %bitcast.225, f32[512,2048]{1,0:T(8,128)S(1)} %copy-done.4, f32[512,2048]{1,0:T(8,128)S(1)} %copy-done.2, f32[128,8,8,128]{3,2,1,0:T(8,128)S(1)} %bitcast.224, ...), kind=kLoop, calls=%fused_computation.48 | loop fusion | flops 11533312 | bytes 23076864 | tf_op jit(solution)/shard_map/reduce_sum | solution.py:284
  426.6 6.7 %convolution_convert_fusion = bf16[1536,1024]{1,0:T(8,128)(2,1)} fusion(bf16[1024,1536]{1,0:T(8,128)(2,1)S(1)} %copy-done.84, bf16[1024,1024]{1,0:T(8,128)(2,1)} %constant_dynamic-update-slice_fusion), kind=kOutput, calls=%fused_computation.70 | convolution fusion | flops 3222798336 | bytes 8388608 | tf_op jit(solution)/shard_map/dot_general | solution.py:52
  437.9 6.5 %convolution_convert_fusion.2 = bf16[1024,1536]{1,0:T(8,128)(2,1)S(1)} fusion(bf16[1024,1536]{1,0:T(8,128)(2,1)} %copy-done.83, bf16[512,1024]{1,0:T(8,128)(2,1)} %collective-permute-done.2, bf16[512,1024]{1,0:T(8,128)(2,1)} %multiply_convert_fusion.4), kind=kOutput, calls=%fused_computation.72 | convolution fusion | flops 3226992640 | bytes 8388608 | tf_op jit(solution)/shard_map/dot_general | solution.py:52
  467.8 19.8 %collective-permute-done.7 = bf16[512,1024]{1,0:T(8,128)(2,1)S(1)} collective-permute-done((bf16[512,1024]{1,0:T(8,128)(2,1)S(1)}, bf16[512,1024]{1,0:T(8,128)(2,1)S(1)}, u32[]{:S(2)}, u32[]{:S(2)}) %collective-permute-start.7) | collective-permute-done | bytes 1048608 | tf_op jit(solution)/shard_map/ppermute | solution.py:170
  491.9 15.5 %collective-permute-done.8 = f32[18,128]{1,0:T(8,128)S(1)} collective-permute-done((f32[18,128]{1,0:T(8,128)S(1)}, f32[18,128]{1,0:T(8,128)S(1)}, u32[]{:S(2)}, u32[]{:S(2)}) %collective-permute-start.8) | collective-permute-done | bytes 9248 | tf_op jit(solution)/shard_map/ppermute | solution.py:139
  526.2 97.4 %reduce-scatter.5.cloned.1.call-done = bf16[64,4608]{1,0:T(8,128)(2,1)} async-done(((bf16[1024,4608]{1,0:T(8,128)(2,1)}), bf16[64,4608]{1,0:T(8,128)(2,1)}) %reduce-scatter.5.cloned.1.call-update) | async-done | bytes 589840 | tf_op jit(solution)/shard_map/reduce_scatter | solution.py:270
  (354 shorter events, 215.6 us)
Async XLA Ops:
  7.2 67.8 %all-gather.3.cloned.1.call-start = ((), (), s32[]{:S(2)}) async-start(), calls=%async_computation.2 | async-start | bytes 6684672 | tf_op jit(solution)/shard_map/all_gather | solution.py:206
  9.2 195.9 %all-gather.5.cloned.1.call-start = ((), (), s32[]{:S(2)}) async-start(), calls=%async_computation.3 | async-start | bytes 10027008 | tf_op jit(solution)/shard_map/all_gather | solution.py:207
  10.3 64.8 %copy-start.74 = (f32[1024]{0:T(1024)S(1)}, f32[1024]{0:T(1024)}, u32[]{:S(2)}) copy-start(f32[1024]{0:T(1024)} %param.28) | copy-start | bytes 12292
  12.2 510.6 %reduce-scatter.3.cloned.1.call-start = ((), (), s32[]{:S(2)}) async-start(), calls=%async_computation.4 | async-start | bytes 6684672 | tf_op jit(solution)/shard_map/reduce_scatter | solution.py:307
  12.2 26.2 %collective-permute-start = (bf16[512,1024]{1,0:T(8,128)(2,1)S(1)}, bf16[512,1024]{1,0:T(8,128)(2,1)S(1)}, u32[]{:S(2)}, u32[]{:S(2)}) collective-permute-start(bf16[512,1024]{1,0:T(8,128)(2,1)S(1)} %copy-done.40), channel_id=1, source_target_pairs={{0,1},{1,0},{2,3},{3,2},{4,5},{5,4},{6,7},{7,6},{8,9},{9,8},{10,11... | collective-permute-start | bytes 3145736 | tf_op jit(solution)/shard_map/ppermute | solution.py:150
  20.3 79.7 %copy-start.15 = (f32[1024,64]{1,0:T(8,128)}, f32[1024,64]{1,0:T(8,128)S(1)}, u32[]{:S(2)}) copy-start(f32[1024,64]{1,0:T(8,128)S(1)} %get-tuple-element.125) | copy-start | bytes 786436
  20.3 79.7 %copy-start.34 = (f32[1024,64]{1,0:T(8,128)}, f32[1024,64]{1,0:T(8,128)S(1)}, u32[]{:S(2)}) copy-start(f32[1024,64]{1,0:T(8,128)S(1)} %get-tuple-element.124) | copy-start | bytes 786436
  38.5 46.6 %copy-start.44 = (bf16[512,1024]{1,0:T(8,128)(2,1)}, bf16[512,1024]{1,0:T(8,128)(2,1)S(1)}, u32[]{:S(2)}) copy-start(bf16[512,1024]{1,0:T(8,128)(2,1)S(1)} %collective-permute-done) | copy-start | bytes 3145732
  117.9 161.4 %copy-start.60 = (f32[1024,4]{0,1:T(4,128)}, f32[1024,4]{0,1:T(4,128)S(1)}, u32[]{:S(2)}) copy-start(f32[1024,4]{0,1:T(4,128)S(1)} %add_rsqrt_fusion.1) | copy-start | bytes 49156
  155.5 26.1 %collective-permute-start.1 = (bf16[512,1024]{1,0:T(8,128)(2,1)S(1)}, bf16[512,1024]{1,0:T(8,128)(2,1)S(1)}, u32[]{:S(2)}, u32[]{:S(2)}) collective-permute-start(bf16[512,1024]{1,0:T(8,128)(2,1)S(1)} %fusion.84), channel_id=1, source_target_pairs={{0,1},{1,0},{2,3},{3,2},{4,5},{5,4},{6,7},{7,6},{8,9},{9,8},{10,11... | collective-permute-start | bytes 3145736 | tf_op jit(solution)/shard_map/ppermute | solution.py:170
  157.1 46.9 %collective-permute-start.4 = (bf16[512,1024]{1,0:T(8,128)(2,1)S(1)}, bf16[512,1024]{1,0:T(8,128)(2,1)S(1)}, u32[]{:S(2)}, u32[]{:S(2)}) collective-permute-start(bf16[512,1024]{1,0:T(8,128)(2,1)S(1)} %copy-done.23), channel_id=1, source_target_pairs={{0,1},{1,0},{2,3},{3,2},{4,5},{5,4},{6,7},{7,6},{8,9},{9,8},{10,11... | collective-permute-start | bytes 3145736 | tf_op jit(solution)/shard_map/ppermute | solution.py:150
  184.7 91.4 %copy-start.10 = (f32[512,1024]{1,0:T(8,128)}, f32[512,1024]{1,0:T(8,128)S(1)}, u32[]{:S(2)}) copy-start(f32[512,1024]{1,0:T(8,128)S(1)} %get-tuple-element.131) | copy-start | bytes 6291460
  184.7 91.4 %copy-start.65 = (f32[512]{0:T(512)}, f32[512]{0:T(512)S(1)}, u32[]{:S(2)}) copy-start(f32[512]{0:T(512)S(1)} %add_rsqrt_fusion.3) | copy-start | bytes 6148
  186.3 39.6 %collective-permute-start.2 = (bf16[512,1024]{1,0:T(8,128)(2,1)}, bf16[512,1024]{1,0:T(8,128)(2,1)}, u32[]{:S(2)}, u32[]{:S(2)}) collective-permute-start(bf16[512,1024]{1,0:T(8,128)(2,1)} %multiply_convert_fusion.4), channel_id=1, source_target_pairs={{0,1},{1,0},{2,3},{3,2},{4,5},{5,4},{6,7},{7,6},{8,9},{9,8},{10,11... | collective-permute-start | bytes 3145736 | tf_op jit(solution)/shard_map/ppermute | solution.py:150
  248.8 24.5 %collective-permute-start.5 = (bf16[512,1024]{1,0:T(8,128)(2,1)S(1)}, bf16[512,1024]{1,0:T(8,128)(2,1)S(1)}, u32[]{:S(2)}, u32[]{:S(2)}) collective-permute-start(bf16[512,1024]{1,0:T(8,128)(2,1)S(1)} %add_convert_fusion.1), channel_id=1, source_target_pairs={{0,1},{1,0},{2,3},{3,2},{4,5},{5,4},{6,7},{7,6},{8,9},{9,8},{10,11... | collective-permute-start | bytes 3145736 | tf_op jit(solution)/shard_map/ppermute | solution.py:170
  277.8 23.8 %collective-permute-start.6 = (bf16[512,1024]{1,0:T(8,128)(2,1)}, bf16[512,1024]{1,0:T(8,128)(2,1)S(1)}, u32[]{:S(2)}, u32[]{:S(2)}) collective-permute-start(bf16[512,1024]{1,0:T(8,128)(2,1)} %fusion.128), channel_id=1, source_target_pairs={{0,1},{1,0},{2,3},{3,2},{4,5},{5,4},{6,7},{7,6},{8,9},{9,8},{10,11... | collective-permute-start | bytes 3145736 | tf_op jit(solution)/shard_map/ppermute | solution.py:150
  424.7 198.9 %reduce-scatter.5.cloned.1.call-start = ((), (), s32[]{:S(2)}) async-start(), calls=%async_computation.5 | async-start | bytes 10027008 | tf_op jit(solution)/shard_map/reduce_scatter | solution.py:270
  461.5 26.1 %collective-permute-start.7 = (bf16[512,1024]{1,0:T(8,128)(2,1)S(1)}, bf16[512,1024]{1,0:T(8,128)(2,1)S(1)}, u32[]{:S(2)}, u32[]{:S(2)}) collective-permute-start(bf16[512,1024]{1,0:T(8,128)(2,1)S(1)} %fusion.87), channel_id=1, source_target_pairs={{0,1},{1,0},{2,3},{3,2},{4,5},{5,4},{6,7},{7,6},{8,9},{9,8},{10,11... | collective-permute-start | bytes 3145736 | tf_op jit(solution)/shard_map/ppermute | solution.py:170
  466.1 44.4 %collective-permute-start.3 = (bf16[512,1024]{1,0:T(8,128)(2,1)S(1)}, bf16[512,1024]{1,0:T(8,128)(2,1)S(1)}, u32[]{:S(2)}, u32[]{:S(2)}) collective-permute-start(bf16[512,1024]{1,0:T(8,128)(2,1)S(1)} %fusion.81), channel_id=1, source_target_pairs={{0,1},{1,0},{2,3},{3,2},{4,5},{5,4},{6,7},{7,6},{8,9},{9,8},{10,11... | collective-permute-start | bytes 3145736 | tf_op jit(solution)/shard_map/ppermute | solution.py:170
  490.3 17.1 %collective-permute-start.8 = (f32[18,128]{1,0:T(8,128)S(1)}, f32[18,128]{1,0:T(8,128)S(1)}, u32[]{:S(2)}, u32[]{:S(2)}) collective-permute-start(f32[18,128]{1,0:T(8,128)S(1)} %maximum_bitcast_fusion.3), channel_id=1, source_target_pairs={{0,1},{1,0},{2,3},{3,2},{4,5},{5,4},{6,7},{7,6},{8,9},{9,8},{10,11... | collective-permute-start | bytes 27656 | tf_op jit(solution)/shard_map/ppermute | solution.py:139
  507.5 1.2 collective-permute-start.9
  508.7 4.6 collective-permute-start.10
  513.3 3.7 collective-permute-start.11
  517.0 4.6 collective-permute-start.12
  (99 other events, 872.0 us)
Sparse Core Ops, SparseCore 0:
  10.9 64.1 all-gather.2
  77.3 79.5 all-gather.4
  424.8 84.4 reduce-scatter.2
  513.3 110.3 reduce-scatter.4
where the time goes:
time: 643 us; the launch traced here: 634 us
  waiting for transfers between devices  274 us (43%)
  matrix products  152 us (24%)
  other arithmetic  101 us (16%)
  local copies, waits for them, and re-layouts  70.6 us (11%)
  starting transfers between devices  19.5 us (3%)
  between operations  15.5 us (2%)
    reduce_scatter x1, waiting for transfers between devices, local(): lax.psum_scatter(grad_mlp_w, 'dp', scatter_dimension=0, tiled=True)  97.4 us
    ppermute x4, waiting for transfers between devices, scatter_rows(): got = lax.ppermute(sent, 'tensor', swap)  64.9 us
    ppermute x4, waiting for transfers between devices, gather_rows(): return jnp.concatenate((own, lax.ppermute(own, 'tensor', swap)), 0)  56.4 us
    dot_general x7, matrix products, matmul(): return jnp.dot(left, right, preferred_element_type=F32)  40.6 us
    all_gather x1, waiting for transfers between devices, local(): full_attn = lax.all_gather(shard_attn, 'dp', axis=0, tiled=True)  36.1 us
    dot_general x8, matrix products, contract_cols(): lax.dot_general(left, right, (((1,), (1,)), ((), ())), preferred_element_...  29.2 us
    dot_general x5, matrix products, contract_rows(): lax.dot_general(left, right, (((0,), (0,)), ((), ())), preferred_element_...  28.4 us
    unnamed x213, local copies, waits for them, and re-layouts  23.4 us
  transfers between devices with their start and end apart: 17, of which 13 were waited for; matrix products, arithmetic and copies ran while one was open for 26% of the time, Pallas kernels for 0%

commit v1 on v0

--- a/solution.py
+++ b/solution.py
@@ -9,6 +9,17 @@
 THETA = 1000000.0
 BF = jnp.bfloat16
 F32 = jnp.float32
+
+
+def gather_by_hops(array, name, dim):
+    count = lax.axis_size(name)
+    right = [(i, (i + 1) % count) for i in range(count)]
+    parts = [array]
+    for far in range(1, count):
+        parts = [lax.ppermute(parts[0], name, right), *parts]
+    whole = jnp.concatenate(parts, axis=dim)
+    shift = (lax.axis_index(name) + 1) * parts[-1].shape[dim]
+    return jnp.roll(whole, shift, axis=dim)
 
 
 def rotary_tables(positions, width):
@@ -203,7 +214,7 @@
             (query_proj, key_proj, value_proj, out_proj.reshape(shard_rows, -1)), 1
         )
         shard_mlp = jnp.concatenate((gate_proj, up_proj, down_proj.reshape(shard_rows, -1)), 1)
-        full_attn = lax.all_gather(shard_attn, "dp", axis=0, tiled=True)
+        full_attn = gather_by_hops(shard_attn, "dp", 0)
         full_mlp = lax.all_gather(shard_mlp, "dp", axis=0, tiled=True)
         proj_qkv = full_attn[:, :width_qkv]
         full_out = full_attn[:, width_qkv:].reshape(-1, width)

time: 643 us -> 730 us (1.14)
  waiting for transfers between devices: 274 us -> 350 us
  local copies, waits for them, and re-layouts: 70.6 us -> 86.5 us
    ppermute x0 -> x15, waiting for transfers between devices: none -> 151 us  [gather_by_hops(): parts = [lax.ppermute(parts[0], name, right), *parts]]
    all_gather x1 -> x0, waiting for transfers between devices: 36.1 us -> none  [local(): full_attn = lax.all_gather(shard_attn, 'dp', axis=0, tiled=True)]
    ppermute x4, waiting for transfers between devices: 56.4 us -> 22.1 us  [gather_rows(): return jnp.concatenate((own, lax.ppermute(own, 'tensor', swap)), 0)]
    ppermute x4, waiting for transfers between devices: 64.9 us -> 48 us  [scatter_rows(): got = lax.ppermute(sent, 'tensor', swap)]
    unnamed x213 -> x288, local copies, waits for them, and re-layouts: 23.4 us -> 37.7 us
    reduce_scatter x1, waiting for transfers between devices: 97.4 us -> 111 us  [local(): lax.psum_scatter(grad_mlp_w, 'dp', scatter_dimension=0, tiled=True)]
    ppermute x5, waiting for transfers between devices: 19.6 us -> 11.4 us  [all_sum(): lax.ppermute(value, axis, [(i, i ^ step) for i in range(size)])]
  transfers between devices with their start and end apart: 17 -> 31, of which waited for: 13 -> 26; matrix products, arithmetic and copies ran while one was open for 26% -> 24% of each run, Pallas kernels for 0% -> 0%
where the time goes in v1:
time: 730 us; the launch traced here: 725 us
  waiting for transfers between devices  350 us (48%)
  matrix products  151 us (21%)
  other arithmetic  102 us (14%)
  local copies, waits for them, and re-layouts  86.5 us (12%)
  starting transfers between devices  18.6 us (3%)
  between operations  15.8 us (2%)
    ppermute x15, waiting for transfers between devices, gather_by_hops(): parts = [lax.ppermute(parts[0], name, right), *parts]  151 us
    reduce_scatter x1, waiting for transfers between devices, local(): lax.psum_scatter(grad_mlp_w, 'dp', scatter_dimension=0, tiled=True)  111 us
    ppermute x4, waiting for transfers between devices, scatter_rows(): got = lax.ppermute(sent, 'tensor', swap)  48 us
    dot_general x7, matrix products, matmul(): return jnp.dot(left, right, preferred_element_type=F32)  38 us
    unnamed x288, local copies, waits for them, and re-layouts  37.7 us
    dot_general x8, matrix products, contract_cols(): lax.dot_general(left, right, (((1,), (1,)), ((), ())), preferred_element_...  31.3 us
    dot_general x5, matrix products, contract_rows(): lax.dot_general(left, right, (((0,), (0,)), ((), ())), preferred_element_...  28.3 us
    ppermute x4, waiting for transfers between devices, gather_rows(): return jnp.concatenate((own, lax.ppermute(own, 'tensor', swap)), 0)  22.1 us
  transfers between devices with their start and end apart: 31, of which 26 were waited for; matrix products, arithmetic and copies ran while one was open for 24% of the time, Pallas kernels for 0%

profile of v1, /device:TPU:0, one launch (start us, length us, event | category | flops | bytes accessed | tf_op | source)
XLA Modules:
  0.0 724.7 jit_solution(12587783999064189599)
XLA Ops:
  8.9 10.4 %collective-permute-done.1 = bf16[64,3072]{1,0:T(8,128)(2,1)S(1)} collective-permute-done((bf16[64,3072]{1,0:T(8,128)(2,1)S(1)}, bf16[64,3072]{1,0:T(8,128)(2,1)S(1)}, u32[]{:S(2)}, u32[]{:S(2)}) %collective-permute-start.1) | collective-permute-done | bytes 393248 | tf_op jit(solution)/shard_map/ppermute | solution.py:19
  19.3 9.9 %collective-permute-done.2 = bf16[64,3072]{1,0:T(8,128)(2,1)S(1)} collective-permute-done((bf16[64,3072]{1,0:T(8,128)(2,1)S(1)}, bf16[64,3072]{1,0:T(8,128)(2,1)S(1)}, u32[]{:S(2)}, u32[]{:S(2)}) %collective-permute-start.2) | collective-permute-done | bytes 393248 | tf_op jit(solution)/shard_map/ppermute | solution.py:19
  29.2 9.9 %collective-permute-done.3 = bf16[64,3072]{1,0:T(8,128)(2,1)S(1)} collective-permute-done((bf16[64,3072]{1,0:T(8,128)(2,1)S(1)}, bf16[64,3072]{1,0:T(8,128)(2,1)S(1)}, u32[]{:S(2)}, u32[]{:S(2)}) %collective-permute-start.3) | collective-permute-done | bytes 393248 | tf_op jit(solution)/shard_map/ppermute | solution.py:19
  39.1 9.9 %collective-permute-done.4 = bf16[64,3072]{1,0:T(8,128)(2,1)S(1)} collective-permute-done((bf16[64,3072]{1,0:T(8,128)(2,1)S(1)}, bf16[64,3072]{1,0:T(8,128)(2,1)S(1)}, u32[]{:S(2)}, u32[]{:S(2)}) %collective-permute-start.4) | collective-permute-done | bytes 393248 | tf_op jit(solution)/shard_map/ppermute | solution.py:19
  49.0 9.9 %collective-permute-done.5 = bf16[64,3072]{1,0:T(8,128)(2,1)S(1)} collective-permute-done((bf16[64,3072]{1,0:T(8,128)(2,1)S(1)}, bf16[64,3072]{1,0:T(8,128)(2,1)S(1)}, u32[]{:S(2)}, u32[]{:S(2)}) %collective-permute-start.5) | collective-permute-done | bytes 393248 | tf_op jit(solution)/shard_map/ppermute | solution.py:19
  58.9 9.9 %collective-permute-done.6 = bf16[64,3072]{1,0:T(8,128)(2,1)S(1)} collective-permute-done((bf16[64,3072]{1,0:T(8,128)(2,1)S(1)}, bf16[64,3072]{1,0:T(8,128)(2,1)S(1)}, u32[]{:S(2)}, u32[]{:S(2)}) %collective-permute-start.6) | collective-permute-done | bytes 393248 | tf_op jit(solution)/shard_map/ppermute | solution.py:19
  68.8 9.9 %collective-permute-done.7 = bf16[64,3072]{1,0:T(8,128)(2,1)S(1)} collective-permute-done((bf16[64,3072]{1,0:T(8,128)(2,1)S(1)}, bf16[64,3072]{1,0:T(8,128)(2,1)S(1)}, u32[]{:S(2)}, u32[]{:S(2)}) %collective-permute-start.7) | collective-permute-done | bytes 393248 | tf_op jit(solution)/shard_map/ppermute | solution.py:19
  78.7 9.9 %collective-permute-done.8 = bf16[64,3072]{1,0:T(8,128)(2,1)S(1)} collective-permute-done((bf16[64,3072]{1,0:T(8,128)(2,1)S(1)}, bf16[64,3072]{1,0:T(8,128)(2,1)S(1)}, u32[]{:S(2)}, u32[]{:S(2)}) %collective-permute-start.8) | collective-permute-done | bytes 393248 | tf_op jit(solution)/shard_map/ppermute | solution.py:19
  88.6 9.9 %collective-permute-done.9 = bf16[64,3072]{1,0:T(8,128)(2,1)S(1)} collective-permute-done((bf16[64,3072]{1,0:T(8,128)(2,1)S(1)}, bf16[64,3072]{1,0:T(8,128)(2,1)S(1)}, u32[]{:S(2)}, u32[]{:S(2)}) %collective-permute-start.9) | collective-permute-done | bytes 393248 | tf_op jit(solution)/shard_map/ppermute | solution.py:19
  98.6 9.9 %collective-permute-done.10 = bf16[64,3072]{1,0:T(8,128)(2,1)S(1)} collective-permute-done((bf16[64,3072]{1,0:T(8,128)(2,1)S(1)}, bf16[64,3072]{1,0:T(8,128)(2,1)S(1)}, u32[]{:S(2)}, u32[]{:S(2)}) %collective-permute-start.10) | collective-permute-done | bytes 393248 | tf_op jit(solution)/shard_map/ppermute | solution.py:19
  108.5 10.0 %collective-permute-done.11 = bf16[64,3072]{1,0:T(8,128)(2,1)} collective-permute-done((bf16[64,3072]{1,0:T(8,128)(2,1)S(1)}, bf16[64,3072]{1,0:T(8,128)(2,1)}, u32[]{:S(2)}, u32[]{:S(2)}) %collective-permute-start.11) | collective-permute-done | bytes 393248 | tf_op jit(solution)/shard_map/ppermute | solution.py:19
  143.8 10.6 %collective-permute-done.14 = bf16[64,3072]{1,0:T(8,128)(2,1)} collective-permute-done((bf16[64,3072]{1,0:T(8,128)(2,1)}, bf16[64,3072]{1,0:T(8,128)(2,1)}, u32[]{:S(2)}, u32[]{:S(2)}) %collective-permute-start.14) | collective-permute-done | bytes 393248 | tf_op jit(solution)/shard_map/ppermute | solution.py:19
  155.7 16.7 %collective-permute-done.15 = bf16[64,3072]{1,0:T(8,128)(2,1)} collective-permute-done((bf16[64,3072]{1,0:T(8,128)(2,1)}, bf16[64,3072]{1,0:T(8,128)(2,1)}, u32[]{:S(2)}, u32[]{:S(2)}) %collective-permute-start.15) | collective-permute-done | bytes 393248 | tf_op jit(solution)/shard_map/ppermute | solution.py:19
  269.3 24.0 %collective-permute-done.16 = bf16[512,1024]{1,0:T(8,128)(2,1)S(1)} collective-permute-done((bf16[512,1024]{1,0:T(8,128)(2,1)S(1)}, bf16[512,1024]{1,0:T(8,128)(2,1)S(1)}, u32[]{:S(2)}, u32[]{:S(2)}) %collective-permute-start.16) | collective-permute-done | bytes 1048608 | tf_op jit(solution)/shard_map/ppermute | solution.py:181
  301.0 10.3 %collective-permute-done.19 = bf16[512,1024]{1,0:T(8,128)(2,1)S(1)} collective-permute-done((bf16[512,1024]{1,0:T(8,128)(2,1)S(1)}, bf16[512,1024]{1,0:T(8,128)(2,1)S(1)}, u32[]{:S(2)}, u32[]{:S(2)}) %collective-permute-start.19) | collective-permute-done | bytes 1048608 | tf_op jit(solution)/shard_map/ppermute | solution.py:161
  322.1 8.7 %fusion.139 = f32[1024,1536]{1,0:T(8,128)} fusion(bf16[1024,1024]{1,0:T(8,128)(2,1)} %constant_dynamic-update-slice_fusion.32, bf16[1536,1024]{1,0:T(8,128)(2,1)} %reshape.389), kind=kOutput, calls=%fused_computation.268 | convolution fusion | flops 3221225472 | bytes 11534336 | tf_op jit(solution)/shard_map/dot_general | solution.py:67
  330.9 8.6 %fusion.42 = f32[1024,1536]{1,0:T(8,128)} fusion(bf16[1024,4608]{1,0:T(8,128)(2,1)} %all-gather.2.cloned.1.call-done, bf16[512,1024]{1,0:T(8,128)(2,1)} %collective-permute-done.17, bf16[512,1024]{1,0:T(8,128)(2,1)} %multiply_convert_fusion.4), kind=kOutput, calls=%fused_computation.83 | convolution fusion | flops 3225419776 | bytes 11534336 | tf_op jit(solution)/shard_map/dot_general | solution.py:59
  339.5 10.9 %multiply_convert_fusion.1 = (bf16[1024,1536]{1,0:T(8,128)(2,1)S(1)}, bf16[1024,1536]{1,0:T(8,128)(2,1)}, bf16[1024,1536]{1,0:T(8,128)(2,1)S(1)}) fusion(f32[1024,1536]{1,0:T(8,128)} %fusion.139, f32[1024,1536]{1,0:T(8,128)} %fusion.42, bf16[1024,4608]{1,0:T(8,128)(2,1)S(1)} %bitcast.242, bf16[512,1024]{1,0:T(8,128)(2,1)} %collective-permute-done.17, ...), kind=kOutput, calls=%fused_computation.34 | convolution fusion | flops 3250585600 | bytes 27262976 | tf_op jit(solution)/shard_map/dot_general | solution.py:59
  357.7 15.7 %collective-permute-done.20 = bf16[512,1024]{1,0:T(8,128)(2,1)S(1)} collective-permute-done((bf16[512,1024]{1,0:T(8,128)(2,1)S(1)}, bf16[512,1024]{1,0:T(8,128)(2,1)S(1)}, u32[]{:S(2)}, u32[]{:S(2)}) %collective-permute-start.20) | collective-permute-done | bytes 1048608 | tf_op jit(solution)/shard_map/ppermute | solution.py:181
  381.1 11.8 %collective-permute-done.21 = bf16[512,1024]{1,0:T(8,128)(2,1)S(1)} collective-permute-done((bf16[512,1024]{1,0:T(8,128)(2,1)}, bf16[512,1024]{1,0:T(8,128)(2,1)S(1)}, u32[]{:S(2)}, u32[]{:S(2)}) %collective-permute-start.21) | collective-permute-done | bytes 1048608 | tf_op jit(solution)/shard_map/ppermute | solution.py:161
  410.5 11.3 %fusion = (f32[4,2,512]{2,1,0:T(2,128)}, f32[4,1024,512,2]{2,1,3,0:T(8,128)}) fusion(f32[4,2,512,1024]{2,3,1,0:T(8,128)S(1)} %bitcast.217, f32[4,2,512]{2,1,0:T(2,128)} %bitcast.246, bf16[512,4,2,128]{0,3,2,1:T(8,128)(2,1)} %bitcast.230, bf16[1024,4,128,1]{2,1,0,3:T(4,128)(2,1)} %bitcast.236), kind=kOutput, calls=%fused_computation.2 | convolution fusion | flops 1086320640 | bytes 35684352 | tf_op jit(solution)/shard_map/qgrd,kgd->grqk/dot_general | solution.py:124
  447.2 16.9 %multiply_reduce_fusion = (f32[1024,8]{1,0:T(8,128)S(1)}, f32[1024,8,128]{2,1,0:T(8,128)}) fusion(f32[1024,8,128]{2,1,0:T(8,128)S(1)} %bitcast.221, f32[128]{0:T(128)S(1)} %copy-done.93, f32[1024,8]{1,0:T(8,128)S(1)} %copy-done.26, f32[1024,8,64]{2,1,0:T(8,128)S(1)} %get-tuple-element.89, f32[1024,8,64]{2,1,0:T(8,128)S(1)} %get-tuple-element.88), kind=kLoop, calls=%fused_computation.57 | loop fusion | flops 5234688 | bytes 12648960 | tf_op jit(solution)/shard_map/reduce_sum | solution.py:54
  472.8 9.9 %fusion.59 = bf16[1024,4,128]{0,2,1:T(8,128)(2,1)} fusion(f32[512,4,128]{0,2,1:T(8,128)} %fusion.100, bf16[512,4,2,128]{0,3,2,1:T(8,128)(2,1)S(1)} %bitcast.231, f32[4,2,512,1024]{2,3,1,0:T(8,128)} %get-tuple-element.129, f32[4,2,512]{2,1,0:T(2,128)S(1)} %bitcast.248), kind=kOutput, calls=%fused_computation.112 | convolution fusion | flops 1083179008 | bytes 19939328 | tf_op jit(solution)/shard_map/grqk,qgrd->kgd/dot_general | solution.py:138
  604.0 110.9 %reduce-scatter.5.cloned.1.call-done = bf16[64,4608]{1,0:T(8,128)(2,1)} async-done(((bf16[1024,4608]{1,0:T(8,128)(2,1)}), bf16[64,4608]{1,0:T(8,128)(2,1)}) %reduce-scatter.5.cloned.1.call-update) | async-done | bytes 589840 | tf_op jit(solution)/shard_map/reduce_scatter | solution.py:281
  (455 shorter events, 333.2 us)
Async XLA Ops:
  7.2 305.1 %all-gather.2.cloned.1.call-start = ((), (), s32[]{:S(2)}) async-start(), calls=%async_computation.2 | async-start | bytes 10027008 | tf_op jit(solution)/shard_map/all_gather | solution.py:218
  8.4 11.0 %collective-permute-start.1 = (bf16[64,3072]{1,0:T(8,128)(2,1)S(1)}, bf16[64,3072]{1,0:T(8,128)(2,1)S(1)}, u32[]{:S(2)}, u32[]{:S(2)}) collective-permute-start(bf16[64,3072]{1,0:T(8,128)(2,1)S(1)} %pad_maximum_fusion.14), channel_id=1, source_target_pairs={{0,2},{2,4},{4,6},{6,8},{8,10},{10,12},{12,14},{14,16},{16,18},{18... | collective-permute-start | bytes 1179656 | tf_op jit(solution)/shard_map/ppermute | solution.py:19
  29.2 9.9 %collective-permute-start.3 = (bf16[64,3072]{1,0:T(8,128)(2,1)S(1)}, bf16[64,3072]{1,0:T(8,128)(2,1)S(1)}, u32[]{:S(2)}, u32[]{:S(2)}) collective-permute-start(bf16[64,3072]{1,0:T(8,128)(2,1)S(1)} %collective-permute-done.2), channel_id=1, source_target_pairs={{0,2},{2,4},{4,6},{6,8},{8,10},{10,12},{12,14},{14,16},{16,18},{18... | collective-permute-start | bytes 1179656 | tf_op jit(solution)/shard_map/ppermute | solution.py:19
  39.1 9.9 %collective-permute-start.4 = (bf16[64,3072]{1,0:T(8,128)(2,1)S(1)}, bf16[64,3072]{1,0:T(8,128)(2,1)S(1)}, u32[]{:S(2)}, u32[]{:S(2)}) collective-permute-start(bf16[64,3072]{1,0:T(8,128)(2,1)S(1)} %collective-permute-done.3), channel_id=1, source_target_pairs={{0,2},{2,4},{4,6},{6,8},{8,10},{10,12},{12,14},{14,16},{16,18},{18... | collective-permute-start | bytes 1179656 | tf_op jit(solution)/shard_map/ppermute | solution.py:19
  49.0 9.9 %collective-permute-start.5 = (bf16[64,3072]{1,0:T(8,128)(2,1)S(1)}, bf16[64,3072]{1,0:T(8,128)(2,1)S(1)}, u32[]{:S(2)}, u32[]{:S(2)}) collective-permute-start(bf16[64,3072]{1,0:T(8,128)(2,1)S(1)} %collective-permute-done.4), channel_id=1, source_target_pairs={{0,2},{2,4},{4,6},{6,8},{8,10},{10,12},{12,14},{14,16},{16,18},{18... | collective-permute-start | bytes 1179656 | tf_op jit(solution)/shard_map/ppermute | solution.py:19
  58.9 9.9 %collective-permute-start.6 = (bf16[64,3072]{1,0:T(8,128)(2,1)S(1)}, bf16[64,3072]{1,0:T(8,128)(2,1)S(1)}, u32[]{:S(2)}, u32[]{:S(2)}) collective-permute-start(bf16[64,3072]{1,0:T(8,128)(2,1)S(1)} %collective-permute-done.5), channel_id=1, source_target_pairs={{0,2},{2,4},{4,6},{6,8},{8,10},{10,12},{12,14},{14,16},{16,18},{18... | collective-permute-start | bytes 1179656 | tf_op jit(solution)/shard_map/ppermute | solution.py:19
  68.8 9.9 %collective-permute-start.7 = (bf16[64,3072]{1,0:T(8,128)(2,1)S(1)}, bf16[64,3072]{1,0:T(8,128)(2,1)S(1)}, u32[]{:S(2)}, u32[]{:S(2)}) collective-permute-start(bf16[64,3072]{1,0:T(8,128)(2,1)S(1)} %collective-permute-done.6), channel_id=1, source_target_pairs={{0,2},{2,4},{4,6},{6,8},{8,10},{10,12},{12,14},{14,16},{16,18},{18... | collective-permute-start | bytes 1179656 | tf_op jit(solution)/shard_map/ppermute | solution.py:19
  78.7 9.9 %collective-permute-start.8 = (bf16[64,3072]{1,0:T(8,128)(2,1)S(1)}, bf16[64,3072]{1,0:T(8,128)(2,1)S(1)}, u32[]{:S(2)}, u32[]{:S(2)}) collective-permute-start(bf16[64,3072]{1,0:T(8,128)(2,1)S(1)} %collective-permute-done.7), channel_id=1, source_target_pairs={{0,2},{2,4},{4,6},{6,8},{8,10},{10,12},{12,14},{14,16},{16,18},{18... | collective-permute-start | bytes 1179656 | tf_op jit(solution)/shard_map/ppermute | solution.py:19
  88.6 9.9 %collective-permute-start.9 = (bf16[64,3072]{1,0:T(8,128)(2,1)S(1)}, bf16[64,3072]{1,0:T(8,128)(2,1)S(1)}, u32[]{:S(2)}, u32[]{:S(2)}) collective-permute-start(bf16[64,3072]{1,0:T(8,128)(2,1)S(1)} %collective-permute-done.8), channel_id=1, source_target_pairs={{0,2},{2,4},{4,6},{6,8},{8,10},{10,12},{12,14},{14,16},{16,18},{18... | collective-permute-start | bytes 1179656 | tf_op jit(solution)/shard_map/ppermute | solution.py:19
  108.4 10.0 %collective-permute-start.11 = (bf16[64,3072]{1,0:T(8,128)(2,1)S(1)}, bf16[64,3072]{1,0:T(8,128)(2,1)}, u32[]{:S(2)}, u32[]{:S(2)}) collective-permute-start(bf16[64,3072]{1,0:T(8,128)(2,1)S(1)} %collective-permute-done.10), channel_id=1, source_target_pairs={{0,2},{2,4},{4,6},{6,8},{8,10},{10,12},{12,14},{14,16},{16,18},{18... | collective-permute-start | bytes 1179656 | tf_op jit(solution)/shard_map/ppermute | solution.py:19
  118.5 10.3 %collective-permute-start.12 = (bf16[64,3072]{1,0:T(8,128)(2,1)}, bf16[64,3072]{1,0:T(8,128)(2,1)}, u32[]{:S(2)}, u32[]{:S(2)}) collective-permute-start(bf16[64,3072]{1,0:T(8,128)(2,1)} %collective-permute-done.11), channel_id=1, source_target_pairs={{0,2},{2,4},{4,6},{6,8},{8,10},{10,12},{12,14},{14,16},{16,18},{18... | collective-permute-start | bytes 1179656 | tf_op jit(solution)/shard_map/ppermute | solution.py:19
  118.6 36.6 %collective-permute-start = (bf16[512,1024]{1,0:T(8,128)(2,1)}, bf16[512,1024]{1,0:T(8,128)(2,1)S(1)}, u32[]{:S(2)}, u32[]{:S(2)}) collective-permute-start(bf16[512,1024]{1,0:T(8,128)(2,1)} %param.26), channel_id=1, source_target_pairs={{0,1},{1,0},{2,3},{3,2},{4,5},{5,4},{6,7},{7,6},{8,9},{9,8},{10,11... | collective-permute-start | bytes 3145736 | tf_op jit(solution)/shard_map/ppermute | solution.py:161
  128.7 10.2 %collective-permute-start.13 = (bf16[64,3072]{1,0:T(8,128)(2,1)}, bf16[64,3072]{1,0:T(8,128)(2,1)}, u32[]{:S(2)}, u32[]{:S(2)}) collective-permute-start(bf16[64,3072]{1,0:T(8,128)(2,1)} %collective-permute-done.12), channel_id=1, source_target_pairs={{0,2},{2,4},{4,6},{6,8},{8,10},{10,12},{12,14},{14,16},{16,18},{18... | collective-permute-start | bytes 1179656 | tf_op jit(solution)/shard_map/ppermute | solution.py:19
  130.7 469.8 %reduce-scatter.3.cloned.1.call-start = ((), (), s32[]{:S(2)}) async-start(), calls=%async_computation.3 | async-start | bytes 6684672 | tf_op jit(solution)/shard_map/reduce_scatter | solution.py:318
  138.9 15.4 %collective-permute-start.14 = (bf16[64,3072]{1,0:T(8,128)(2,1)}, bf16[64,3072]{1,0:T(8,128)(2,1)}, u32[]{:S(2)}, u32[]{:S(2)}) collective-permute-start(bf16[64,3072]{1,0:T(8,128)(2,1)} %collective-permute-done.13), channel_id=1, source_target_pairs={{0,2},{2,4},{4,6},{6,8},{8,10},{10,12},{12,14},{14,16},{16,18},{18... | collective-permute-start | bytes 1179656 | tf_op jit(solution)/shard_map/ppermute | solution.py:19
  154.4 18.0 %collective-permute-start.15 = (bf16[64,3072]{1,0:T(8,128)(2,1)}, bf16[64,3072]{1,0:T(8,128)(2,1)}, u32[]{:S(2)}, u32[]{:S(2)}) collective-permute-start(bf16[64,3072]{1,0:T(8,128)(2,1)} %collective-permute-done.14), channel_id=1, source_target_pairs={{0,2},{2,4},{4,6},{6,8},{8,10},{10,12},{12,14},{14,16},{16,18},{18... | collective-permute-start | bytes 1179656 | tf_op jit(solution)/shard_map/ppermute | solution.py:19
  267.2 26.1 %collective-permute-start.16 = (bf16[512,1024]{1,0:T(8,128)(2,1)S(1)}, bf16[512,1024]{1,0:T(8,128)(2,1)S(1)}, u32[]{:S(2)}, u32[]{:S(2)}) collective-permute-start(bf16[512,1024]{1,0:T(8,128)(2,1)S(1)} %fusion.84), channel_id=1, source_target_pairs={{0,1},{1,0},{2,3},{3,2},{4,5},{5,4},{6,7},{7,6},{8,9},{9,8},{10,11... | collective-permute-start | bytes 3145736 | tf_op jit(solution)/shard_map/ppermute | solution.py:181
  269.2 42.0 %collective-permute-start.19 = (bf16[512,1024]{1,0:T(8,128)(2,1)S(1)}, bf16[512,1024]{1,0:T(8,128)(2,1)S(1)}, u32[]{:S(2)}, u32[]{:S(2)}) collective-permute-start(bf16[512,1024]{1,0:T(8,128)(2,1)S(1)} %copy-done.22), channel_id=1, source_target_pairs={{0,1},{1,0},{2,3},{3,2},{4,5},{5,4},{6,7},{7,6},{8,9},{9,8},{10,11... | collective-permute-start | bytes 3145736 | tf_op jit(solution)/shard_map/ppermute | solution.py:161
  297.9 32.9 %collective-permute-start.17 = (bf16[512,1024]{1,0:T(8,128)(2,1)}, bf16[512,1024]{1,0:T(8,128)(2,1)}, u32[]{:S(2)}, u32[]{:S(2)}) collective-permute-start(bf16[512,1024]{1,0:T(8,128)(2,1)} %multiply_convert_fusion.4), channel_id=1, source_target_pairs={{0,1},{1,0},{2,3},{3,2},{4,5},{5,4},{6,7},{7,6},{8,9},{9,8},{10,11... | collective-permute-start | bytes 3145736 | tf_op jit(solution)/shard_map/ppermute | solution.py:161
  354.1 19.3 %collective-permute-start.20 = (bf16[512,1024]{1,0:T(8,128)(2,1)S(1)}, bf16[512,1024]{1,0:T(8,128)(2,1)S(1)}, u32[]{:S(2)}, u32[]{:S(2)}) collective-permute-start(bf16[512,1024]{1,0:T(8,128)(2,1)S(1)} %add_convert_fusion.1), channel_id=1, source_target_pairs={{0,1},{1,0},{2,3},{3,2},{4,5},{5,4},{6,7},{7,6},{8,9},{9,8},{10,11... | collective-permute-start | bytes 3145736 | tf_op jit(solution)/shard_map/ppermute | solution.py:181
  377.9 15.0 %collective-permute-start.21 = (bf16[512,1024]{1,0:T(8,128)(2,1)}, bf16[512,1024]{1,0:T(8,128)(2,1)S(1)}, u32[]{:S(2)}, u32[]{:S(2)}) collective-permute-start(bf16[512,1024]{1,0:T(8,128)(2,1)} %fusion.131), channel_id=1, source_target_pairs={{0,1},{1,0},{2,3},{3,2},{4,5},{5,4},{6,7},{7,6},{8,9},{9,8},{10,11... | collective-permute-start | bytes 3145736 | tf_op jit(solution)/shard_map/ppermute | solution.py:161
  515.1 199.9 %reduce-scatter.5.cloned.1.call-start = ((), (), s32[]{:S(2)}) async-start(), calls=%async_computation.4 | async-start | bytes 10027008 | tf_op jit(solution)/shard_map/reduce_scatter | solution.py:281
  551.7 14.9 %collective-permute-start.22 = (bf16[512,1024]{1,0:T(8,128)(2,1)S(1)}, bf16[512,1024]{1,0:T(8,128)(2,1)S(1)}, u32[]{:S(2)}, u32[]{:S(2)}) collective-permute-start(bf16[512,1024]{1,0:T(8,128)(2,1)S(1)} %fusion.87), channel_id=1, source_target_pairs={{0,1},{1,0},{2,3},{3,2},{4,5},{5,4},{6,7},{7,6},{8,9},{9,8},{10,11... | collective-permute-start | bytes 3145736 | tf_op jit(solution)/shard_map/ppermute | solution.py:181
  556.3 22.9 %collective-permute-start.18 = (bf16[512,1024]{1,0:T(8,128)(2,1)S(1)}, bf16[512,1024]{1,0:T(8,128)(2,1)S(1)}, u32[]{:S(2)}, u32[]{:S(2)}) collective-permute-start(bf16[512,1024]{1,0:T(8,128)(2,1)S(1)} %fusion.81), channel_id=1, source_target_pairs={{0,1},{1,0},{2,3},{3,2},{4,5},{5,4},{6,7},{7,6},{8,9},{9,8},{10,11... | collective-permute-start | bytes 3145736 | tf_op jit(solution)/shard_map/ppermute | solution.py:181
  (131 other events, 2110.0 us)
Sparse Core Ops, SparseCore 0:
  130.9 89.1 all-gather.1
  515.2 85.3 reduce-scatter.2
  604.7 110.2 reduce-scatter.4
